TPU v7x, 256 devices: a whole 4x4x8 slice. The times are simulated.
256 devices in a mesh: seq: 16 (over z, core), head: 16 (over x, y).
Axes of the slice: x: 4, y: 4, z: 8, core: 2. Of those that a mesh axis runs over, the one named last changes fastest.
Arguments:
- features: bfloat16 [65536, 8192], P(('seq', 'head')), may hold values from -6 to 6
- step_size: float32 [65536, 128], P(('seq', 'head')), may hold values from 0.01 to 0.08
- log_decay: float32 [65536, 128], P(('seq', 'head')), may hold values from -0.6 to 0
- inject: bfloat16 [65536, 1024], P(('seq', 'head')), may hold values from -1.5 to 1.5
- readout: bfloat16 [65536, 1024], P(('seq', 'head')), may hold values from -1.5 to 1.5
- skip_gain: float32 [128], replicated, may hold values from 0.5 to 1.5
Outputs:
- mixer_out: bfloat16 [65536, 8192], P(('seq', 'head'))
All inputs are finite; a program needn't handle non-finite values.
Results may differ from a plain program's by a relative error of at most 0.02.
Values may be sent and summed in bfloat16 or wider, within the bound.
No kernel may reach another device: no remote copies, remote signals or barrier semaphores. Data moves between devices by JAX's collectives and lax.ppermute only.
A program may use at most 128 MiB of HBM per device.

v0:
```python
import jax
import jax.numpy as jnp
from jax import lax
from jax.sharding import PartitionSpec as P

HEAD_DIM = 64
STATE = 128
GROUPS = 8
SPAN = 512


def entering_2(x, axis, join, neutral):
    place = lax.axis_index(axis)
    gathered = jax.tree.map(
        lambda a, kind: lax.all_gather(a.astype(kind), axis), x, (jnp.bfloat16, jnp.bfloat16)
    )
    state = jax.tree.map(lambda a, e: jnp.zeros_like(a) + jnp.asarray(e, a.dtype), x, neutral)

    def one(step, state):
        return join(
            state,
            jax.tree.map(
                lambda a, own: lax.dynamic_index_in_dim(a, step, 0, False).astype(own.dtype),
                gathered,
                x,
            ),
        )

    return lax.fori_loop(0, place, one, state)


def shards(features, step_size, log_decay, inject, readout, skip_gain):
    head_ways = lax.axis_size("head")
    head_index = lax.axis_index("head")
    heads_all = step_size.shape[1]
    local_heads = heads_all // head_ways
    group_heads = heads_all // GROUPS
    local_groups = max(1, local_heads // group_heads)
    per_group = local_heads // local_groups
    regrouped = lax.all_to_all(features, "head", split_axis=1, concat_axis=0, tiled=True)
    steps_local, decay_local = (
        lax.all_to_all(
            step_size.astype(jnp.bfloat16), "head", split_axis=1, concat_axis=0, tiled=True
        ).astype(step_size.dtype),
        lax.all_to_all(
            log_decay.astype(jnp.bfloat16), "head", split_axis=1, concat_axis=0, tiled=True
        ).astype(log_decay.dtype),
    )
    inject_all, readout_all = (
        lax.all_gather(inject, "head", axis=0, tiled=True),
        lax.all_gather(readout, "head", axis=0, tiled=True),
    )
    first_col = head_index * local_heads // group_heads * STATE
    inject_mine = lax.dynamic_slice_in_dim(inject_all, first_col, local_groups * STATE, 1)
    readout_mine = lax.dynamic_slice_in_dim(readout_all, first_col, local_groups * STATE, 1)
    seq_rows = regrouped.shape[0]
    spans = seq_rows // SPAN
    drive = (
        regrouped.reshape(seq_rows, local_heads, HEAD_DIM).astype(jnp.float32)
        * steps_local[:, :, None]
    ).astype(jnp.bfloat16)
    drive_q = drive.reshape(spans, SPAN, local_groups, per_group, HEAD_DIM)
    cum_q = jnp.cumsum(decay_local.reshape(spans, SPAN, local_heads), axis=1)
    inject_q = inject_mine.reshape(spans, SPAN, local_groups, STATE)
    readout_q = readout_mine.reshape(spans, SPAN, local_groups, STATE)
    row_ids = lax.broadcasted_iota(jnp.int32, (SPAN, SPAN), 0)
    col_ids = lax.broadcasted_iota(jnp.int32, (SPAN, SPAN), 1)
    lower_mask = row_ids >= col_ids

    def span_terms(pieces):
        read_c, inject_c, drive_c, cum_c = pieces
        intersection = jnp.einsum(
            "ign,jgn->gij", read_c, inject_c, preferred_element_type=jnp.float32
        )
        cum_heads = cum_c.T
        log_gap = cum_heads[:, :, None] - cum_heads[:, None, :]
        decays = jnp.where(lower_mask, jnp.exp(jnp.where(lower_mask, log_gap, 0.0)), 0.0)
        weights = (
            decays.reshape(local_groups, per_group, SPAN, SPAN) * intersection[:, None]
        ).astype(jnp.bfloat16)
        inner_out = jnp.einsum(
            "ghij,jghp->ighp", weights, drive_c, preferred_element_type=jnp.float32
        )
        tail_decay = jnp.exp(cum_heads[:, -1:] - cum_heads)
        scaled = (
            drive_c.astype(jnp.float32)
            * tail_decay.T.reshape(SPAN, local_groups, per_group)[..., None]
        ).astype(jnp.bfloat16)
        summary = jnp.einsum("jghp,jgn->ghpn", scaled, inject_c, preferred_element_type=jnp.float32)
        return (inner_out, summary.reshape(local_heads, HEAD_DIM, STATE))

    inner_out, summary = lax.map(span_terms, (readout_q, inject_q, drive_q, cum_q))
    totals = cum_q[:, -1, :]

    def advance(carried, pieces):
        block_total, summary_c = pieces
        updated = carried * jnp.exp(block_total)[:, None, None] + summary_c
        return (updated, carried)

    zero_state = jnp.zeros((local_heads, HEAD_DIM, STATE), jnp.float32)
    end_state, entering = lax.scan(advance, zero_state, (totals, summary))
    dev_total = jnp.sum(totals, axis=0)

    def combine(earlier, following):
        return (
            earlier[0] + following[0],
            earlier[1] * jnp.exp(following[0])[:, None, None] + following[1],
        )

    identity = (jnp.zeros((local_heads,), jnp.float32), zero_state)
    scanned = entering_2((dev_total, end_state), "seq", combine, identity)
    incoming = scanned[1]
    before = jnp.cumsum(totals, axis=0) - totals
    states = entering + jnp.exp(before)[:, :, None, None] * incoming[None]
    held = states.astype(jnp.bfloat16).reshape(spans, local_groups, per_group, HEAD_DIM, STATE)
    outer_out = jnp.einsum("cign,cghpn->cighp", readout_q, held, preferred_element_type=jnp.float32)
    outer_out = outer_out * jnp.exp(cum_q).reshape(spans, SPAN, local_groups, per_group)[..., None]
    skip_local = lax.dynamic_slice_in_dim(skip_gain, head_index * local_heads, local_heads)
    plain = regrouped.reshape(spans, SPAN, local_groups, per_group, HEAD_DIM).astype(jnp.float32)
    total_out = (
        inner_out + outer_out + skip_local.reshape(local_groups, per_group)[:, :, None] * plain
    )
    mixed_rows = total_out.astype(jnp.bfloat16).reshape(seq_rows, local_heads * HEAD_DIM)
    return lax.all_to_all(mixed_rows, "head", split_axis=0, concat_axis=1, tiled=True)


def solution(mesh):
    placed = (
        P(("seq", "head"), None),
        P(("seq", "head"), None),
        P(("seq", "head"), None),
        P(("seq", "head"), None),
        P(("seq", "head"), None),
        P(),
    )
    return jax.shard_map(
        shards, mesh=mesh, in_specs=placed, out_specs=P(("seq", "head"), None), check_vma=False
    )
```

profile of v0, /device:TPU:225, one launch (start us, length us, event | category | flops | bytes accessed | tf_op | source)
XLA Modules:
  0.0 422.0 jit_solution(15952692852257553255)
XLA Ops:
  8.0 1.6 copy.82
  9.6 6.8 %all-to-all-start.2 = ((bf16[256,16,8]{0,2,1:T(8,128)(2,1)}), bf16[256,16,8]{0,2,1:T(8,128)(2,1)S(1)}, u32[]{:S(2)}, u32[]{:S(2)}) async-start(bf16[256,16,8]{0,2,1:T(8,128)(2,1)} %bitcast.102), calls=%async_computation.2 | async-start | bytes 131072 | tf_op jit(solution)/shard_map/all_to_all | solution.py:45
  16.4 1.6 copy.80
  18.0 4.9 %all-to-all-done.2 = bf16[256,16,8]{0,2,1:T(8,128)(2,1)S(1)} async-done(((bf16[256,16,8]{0,2,1:T(8,128)(2,1)}), bf16[256,16,8]{0,2,1:T(8,128)(2,1)S(1)}, u32[]{:S(2)}, u32[]{:S(2)}) %all-to-all-start.2) | async-done | bytes 65568 | tf_op jit(solution)/shard_map/all_to_all | solution.py:45
  22.9 3.5 all-to-all-start.1
  26.4 6.4 %copy.78 = bf16[256,8192]{0,1:T(8,128)(2,1)} copy(bf16[256,8192]{1,0:T(8,128)(2,1)} %param.12) | data formatting | bytes 8388608 | tf_op args[0]
  33.2 6.3 %all-to-all-start = ((bf16[256,16,512]{0,2,1:T(8,128)(2,1)}), bf16[256,16,512]{0,2,1:T(8,128)(2,1)}, u32[]{:S(2)}, u32[]{:S(2)}) async-start(bf16[256,16,512]{0,2,1:T(8,128)(2,1)} %bitcast.134), calls=%async_computation | async-start | bytes 8388608 | tf_op jit(solution)/shard_map/all_to_all | solution.py:40
  39.6 9.0 %reduce-window.6 = f32[8,8,4,128]{3,1,2,0:T(8,128)S(1)} reduce-window(f32[8,8,4,128]{3,1,2,0:T(8,128)S(1)} %bitcast.139, f32[]{:T(128)} %constant.75.clone.1), window={size=1x1x1x128 pad=0_0x0_0x0_0x127_0}, to_apply=%region_0.1 | reduce-window | flops 4161536 | bytes 262148 | tf_op jit(solution)/shard_map/reduce-window
  49.6 65.2 %all-to-all-done = bf16[256,16,512]{0,2,1:T(8,128)(2,1)} async-done(((bf16[256,16,512]{0,2,1:T(8,128)(2,1)}), bf16[256,16,512]{0,2,1:T(8,128)(2,1)}, u32[]{:S(2)}, u32[]{:S(2)}) %all-to-all-start) | async-done | bytes 4194336 | tf_op jit(solution)/shard_map/all_to_all | solution.py:40
  114.8 3.1 convert_bitcast_fusion
  117.9 8.1 %copy.79 = f32[16,256,512]{1,0,2:T(8,128)} copy(f32[16,256,512]{1,2,0:T(8,128)S(1)} %convert_bitcast_fusion) | data formatting | bytes 16777216 | tf_op jit(solution)/shard_map/convert_element_type | solution.py:59
  125.9 9.8 %reshape.178 = f32[8,512,1,8,64]{1,0,4,3,2:T(8,128)} reshape(f32[16,256,512]{1,0,2:T(8,128)} %copy.79) | data formatting | bytes 16777216 | tf_op jit(solution)/shard_map/convert_element_type | solution.py:59
  135.7 5.1 %multiply_convert_fusion.7 = bf16[8,512,1,8,64]{1,0,4,3,2:T(8,128)(2,1)S(1)} fusion(f32[8,512,1,8,64]{1,0,4,3,2:T(8,128)} %reshape.178, f32[8,512,8]{1,0,2:T(8,128)S(1)} %copy.81), kind=kLoop, calls=%fused_computation.43 | loop fusion | flops 4194304 | bytes 12713984 | tf_op jit(solution)/shard_map/convert_element_type | solution.py:61
  140.8 3.5 copy.85
  144.3 1.3 constant_dynamic-slice_fusion.2
  145.6 54.1 %all-gather.8.cloned.1.call-done = bf16[4096,1024]{1,0:T(8,128)(2,1)} async-done(((bf16[256,1024]{1,0:T(8,128)(2,1)}), bf16[4096,1024]{1,0:T(8,128)(2,1)}) %all-gather.8.cloned.1.call-update) | async-done | bytes 8388624 | tf_op jit(solution)/shard_map/all_gather | solution.py:50
  199.7 1.3 constant_dynamic-slice_fusion.1
  201.0 1.6 broadcast.55.clone
  202.6 59.0 %while.40 = (s32[]{:T(128)}, f32[8,512,1,8,64]{1,4,3,2,0:T(8,128)}, f32[8,8,64,128]{3,2,1,0:T(8,128)}, bf16[8,512,1,8,64]{1,4,3,2,0:T(8,128)(2,1)}, f32[8,512,8]...) while((s32[]{:T(128)}, f32[8,512,1,8,64]{1,4,3,2,0:T(8,128)}, ...), condition=%wide.region_3.4_spmd.clone.clone, body=%wide.region_2.3_spmd.clone.clone.sunk | while | flops 414191616 | bytes 5492413 | solution.py:92
  203.0 4.7 %fusion.52 = f32[8,512,1,8,64]{1,4,3,2,0:T(8,128)} fusion(f32[8,512,1,8,64]{1,4,3,2,0:T(8,128)} %get-tuple-element.377, s32[]{:T(128)} %get-tuple-element.376, f32[512,512]{1,0:T(8,128)S(1)} %fusion.51, f32[8,512]{1,0:T(8,128)S(1)} %dynamic-slice_bitcast_fusion.2, pred[512,512]{1,0:T(8,128)(4,1)S(1)} %iota_compare_fusion.2, ...), kind=kOutput, calls=%fused_computation.12.clone.1 | convolution fusion | flops 278921216 | bytes 2917376 | tf_op jit(solution)/shard_map/while/body/eval_jaxpr/ghij,jghp->ighp/dot_general | solution.py:81
  207.9 2.0 fusion.54
  210.4 4.6 %fusion.52 = f32[8,512,1,8,64]{1,4,3,2,0:T(8,128)} fusion(f32[8,512,1,8,64]{1,4,3,2,0:T(8,128)} %get-tuple-element.377, s32[]{:T(128)} %get-tuple-element.376, f32[512,512]{1,0:T(8,128)S(1)} %fusion.51, f32[8,512]{1,0:T(8,128)S(1)} %dynamic-slice_bitcast_fusion.2, pred[512,512]{1,0:T(8,128)(4,1)S(1)} %iota_compare_fusion.2, ...), kind=kOutput, calls=%fused_computation.12.clone.1 | convolution fusion | flops 278921216 | bytes 2917376 | tf_op jit(solution)/shard_map/while/body/eval_jaxpr/ghij,jghp->ighp/dot_general | solution.py:81
  215.3 2.0 fusion.54
  217.7 4.7 %fusion.52 = f32[8,512,1,8,64]{1,4,3,2,0:T(8,128)} fusion(f32[8,512,1,8,64]{1,4,3,2,0:T(8,128)} %get-tuple-element.377, s32[]{:T(128)} %get-tuple-element.376, f32[512,512]{1,0:T(8,128)S(1)} %fusion.51, f32[8,512]{1,0:T(8,128)S(1)} %dynamic-slice_bitcast_fusion.2, pred[512,512]{1,0:T(8,128)(4,1)S(1)} %iota_compare_fusion.2, ...), kind=kOutput, calls=%fused_computation.12.clone.1 | convolution fusion | flops 278921216 | bytes 2917376 | tf_op jit(solution)/shard_map/while/body/eval_jaxpr/ghij,jghp->ighp/dot_general | solution.py:81
  222.7 2.0 fusion.54
  225.1 4.7 %fusion.52 = f32[8,512,1,8,64]{1,4,3,2,0:T(8,128)} fusion(f32[8,512,1,8,64]{1,4,3,2,0:T(8,128)} %get-tuple-element.377, s32[]{:T(128)} %get-tuple-element.376, f32[512,512]{1,0:T(8,128)S(1)} %fusion.51, f32[8,512]{1,0:T(8,128)S(1)} %dynamic-slice_bitcast_fusion.2, pred[512,512]{1,0:T(8,128)(4,1)S(1)} %iota_compare_fusion.2, ...), kind=kOutput, calls=%fused_computation.12.clone.1 | convolution fusion | flops 278921216 | bytes 2917376 | tf_op jit(solution)/shard_map/while/body/eval_jaxpr/ghij,jghp->ighp/dot_general | solution.py:81
  230.0 2.0 fusion.54
  232.5 4.7 %fusion.52 = f32[8,512,1,8,64]{1,4,3,2,0:T(8,128)} fusion(f32[8,512,1,8,64]{1,4,3,2,0:T(8,128)} %get-tuple-element.377, s32[]{:T(128)} %get-tuple-element.376, f32[512,512]{1,0:T(8,128)S(1)} %fusion.51, f32[8,512]{1,0:T(8,128)S(1)} %dynamic-slice_bitcast_fusion.2, pred[512,512]{1,0:T(8,128)(4,1)S(1)} %iota_compare_fusion.2, ...), kind=kOutput, calls=%fused_computation.12.clone.1 | convolution fusion | flops 278921216 | bytes 2917376 | tf_op jit(solution)/shard_map/while/body/eval_jaxpr/ghij,jghp->ighp/dot_general | solution.py:81
  237.4 2.1 fusion.54
  239.9 4.6 %fusion.52 = f32[8,512,1,8,64]{1,4,3,2,0:T(8,128)} fusion(f32[8,512,1,8,64]{1,4,3,2,0:T(8,128)} %get-tuple-element.377, s32[]{:T(128)} %get-tuple-element.376, f32[512,512]{1,0:T(8,128)S(1)} %fusion.51, f32[8,512]{1,0:T(8,128)S(1)} %dynamic-slice_bitcast_fusion.2, pred[512,512]{1,0:T(8,128)(4,1)S(1)} %iota_compare_fusion.2, ...), kind=kOutput, calls=%fused_computation.12.clone.1 | convolution fusion | flops 278921216 | bytes 2917376 | tf_op jit(solution)/shard_map/while/body/eval_jaxpr/ghij,jghp->ighp/dot_general | solution.py:81
  244.8 2.1 fusion.54
  247.2 4.7 %fusion.52 = f32[8,512,1,8,64]{1,4,3,2,0:T(8,128)} fusion(f32[8,512,1,8,64]{1,4,3,2,0:T(8,128)} %get-tuple-element.377, s32[]{:T(128)} %get-tuple-element.376, f32[512,512]{1,0:T(8,128)S(1)} %fusion.51, f32[8,512]{1,0:T(8,128)S(1)} %dynamic-slice_bitcast_fusion.2, pred[512,512]{1,0:T(8,128)(4,1)S(1)} %iota_compare_fusion.2, ...), kind=kOutput, calls=%fused_computation.12.clone.1 | convolution fusion | flops 278921216 | bytes 2917376 | tf_op jit(solution)/shard_map/while/body/eval_jaxpr/ghij,jghp->ighp/dot_general | solution.py:81
  252.2 2.1 fusion.54
  254.7 4.6 %fusion.52 = f32[8,512,1,8,64]{1,4,3,2,0:T(8,128)} fusion(f32[8,512,1,8,64]{1,4,3,2,0:T(8,128)} %get-tuple-element.377, s32[]{:T(128)} %get-tuple-element.376, f32[512,512]{1,0:T(8,128)S(1)} %fusion.51, f32[8,512]{1,0:T(8,128)S(1)} %dynamic-slice_bitcast_fusion.2, pred[512,512]{1,0:T(8,128)(4,1)S(1)} %iota_compare_fusion.2, ...), kind=kOutput, calls=%fused_computation.12.clone.1 | convolution fusion | flops 278921216 | bytes 2917376 | tf_op jit(solution)/shard_map/while/body/eval_jaxpr/ghij,jghp->ighp/dot_general | solution.py:81
  259.5 2.1 fusion.54
  261.9 8.9 %while.41 = (s32[]{:T(128)}, f32[8,64,128]{2,1,0:T(8,128)S(1)}, f32[8,8,64,128]{3,2,1,0:T(8,128)S(1)}, f32[8,8]{1,0:T(8,128)S(1)}, f32[8,8,64,128]{3,2,1,0:T(8,128)}, /*index=5*/s32[]{:T(128)}, s32[]{:T(128)}) while((s32[]{:T(128)}, f32[8,64,128]{2,1,0:T(8,128)S(1)}, f32[8,8,64,128]{3,2,1,0:T(8,128)S(1)}, f32[8,8]{1,0:T(8,128)S(1)}, ...), condition=%wide.region_5.6_spmd.clone, body=%wide.region_4.5_spmd.clone.sunk | while | flops 262147 | bytes 1310916 | solution.py:101
  261.9 1.0 bitcast_add_fusion.2
  263.1 1.0 bitcast_add_fusion.2
  264.2 1.0 bitcast_add_fusion.2
  265.3 1.0 bitcast_add_fusion.2
  266.4 1.0 bitcast_add_fusion.2
  267.5 1.0 bitcast_add_fusion.2
  268.6 1.0 bitcast_add_fusion.2
  269.8 1.0 bitcast_add_fusion.2
  273.2 23.8 %all-reduce = bf16[128]{0:T(256)(128)(2,1)S(1)} all-reduce(bf16[128]{0:T(256)(128)(2,1)S(1)} %dynamic-update-slice), channel_id=2, replica_groups=mesh['seq'=16,'head'=16] {'seq'}, use_global_device_ids=true, to_apply=%add | all-reduce | flops 128 | bytes 512
  297.1 12.5 %all-gather.10.cloned.1.call-done = bf16[128,64,128]{2,1,0:T(8,128)(2,1)} async-done(((bf16[8,64,128]{2,1,0:T(8,128)(2,1)}), bf16[128,64,128]{2,1,0:T(8,128)(2,1)}) %all-gather.10.cloned.1.call-update) | async-done | bytes 2097168 | tf_op jit(solution)/shard_map/all_gather | solution.py:15
  309.6 16.0 %while.39 = (s32[]{:T(128)}, f32[8,64,128]{2,1,0:T(8,128)S(1)}, s32[]{:T(128)}, bf16[16,8]{1,0:T(8,128)(2,1)S(1)}, bf16[16,8,64,128]{3,2,1,0:T(8,128)(2,1)}, /*index=5*/s32[]{:T(128)}, s32[]{:T(128)}, s32[]{:T(128)}) while((s32[]{:T(128)}, f32[8,64,128]{2,1,0:T(8,128)S(1)}, s32[]{:T(128)}, bf16[16,8]{1,0:T(8,128)(2,1)S(1)}, ...), condition=%wide.region_9.10_spmd, body=%wide.region_8.9_spmd.sunk | while | flops 196621 | bytes 655567 | solution.py:29
  309.6 1.0 convert_add_fusion.2
  310.7 1.0 convert_add_fusion.2
  311.8 1.0 convert_add_fusion.2
  312.8 1.0 convert_add_fusion.2
  313.9 1.0 convert_add_fusion.2
  315.0 1.0 convert_add_fusion.2
  316.0 1.0 convert_add_fusion.2
  318.2 1.0 convert_add_fusion.2
  319.2 1.0 convert_add_fusion.2
  323.5 1.0 convert_add_fusion.2
  324.6 1.0 convert_add_fusion.2
  325.6 10.9 %fusion.29 = bf16[8,512,1,8,64]{1,4,3,0,2:T(8,128)(2,1)S(1)} fusion(f32[8,512,1,8,64]{1,4,3,2,0:T(8,128)} %get-tuple-element.123, f32[8,512,1,8,64]{1,0,4,3,2:T(8,128)} %reshape.178, f32[8]{0:T(128)S(1)} %dynamic_slice.44, f32[8,512,8]{1,2,0:T(8,128)S(1)} %get-tuple-element.260, bf16[8,512,128,1]{2,1,3,0:T(8,128)(2,1)S(1)} %bitcast.137, ...), kind=kOutput, calls=%fused_computation.40 | convolution fusion | flops 548929536 | bytes 24510752 | tf_op jit(solution)/shard_map/cign,cghpn->cighp/dot_general | solution.py:116
  336.5 4.6 %copy.89 = bf16[8,512,1,8,64]{1,0,4,3,2:T(8,128)(2,1)} copy(bf16[8,512,1,8,64]{1,4,3,0,2:T(8,128)(2,1)S(1)} %fusion.29) | data formatting | bytes 8388608 | tf_op jit(solution)/shard_map/convert_element_type | solution.py:123
  341.0 7.1 %all_to_all.50 = bf16[16,256,512]{1,0,2:T(8,128)(2,1)} reshape(bf16[8,512,1,8,64]{1,0,4,3,2:T(8,128)(2,1)} %copy.89) | data formatting | bytes 8388608 | tf_op jit(solution)/shard_map/all_to_all | solution.py:124
  348.1 3.7 copy.90
  351.8 57.4 %all_to_all.58 = bf16[16,256,512]{1,2,0:T(8,128)(2,1)} all-to-all(bf16[16,256,512]{1,2,0:T(8,128)(2,1)S(1)} %copy.90), channel_id=1, replica_groups=mesh['seq'=16,'head'=16] {'head'}, dimensions={0} | all-to-all | bytes 8388608 | tf_op jit(solution)/shard_map/all_to_all | solution.py:124
  409.2 6.3 %copy.91 = bf16[256,8192]{1,0:T(8,128)(2,1)} copy(bf16[256,8192]{0,1:T(8,128)(2,1)} %bitcast.135) | data formatting | bytes 8388608 | tf_op jit(solution)/shard_map/all_to_all | solution.py:124
  (109 shorter events, 14.6 us)
Async XLA Ops:
  6.5 137.8 %all-gather.6.cloned.1.call-start = ((), (), s32[]{:S(2)}) async-start(), calls=%async_computation.4 | async-start | bytes 8912896 | tf_op jit(solution)/shard_map/all_gather | solution.py:51
  7.3 192.4 %all-gather.8.cloned.1.call-start = ((), (), s32[]{:S(2)}) async-start(), calls=%async_computation.5 | async-start | bytes 8912896 | tf_op jit(solution)/shard_map/all_gather | solution.py:50
  9.6 13.3 %all-to-all-start.2 = ((bf16[256,16,8]{0,2,1:T(8,128)(2,1)}), bf16[256,16,8]{0,2,1:T(8,128)(2,1)S(1)}, u32[]{:S(2)}, u32[]{:S(2)}) async-start(bf16[256,16,8]{0,2,1:T(8,128)(2,1)} %bitcast.102), calls=%async_computation.2 | async-start | bytes 131072 | tf_op jit(solution)/shard_map/all_to_all | solution.py:45
  22.9 10.3 %all-to-all-start.1 = ((bf16[256,16,8]{0,2,1:T(8,128)(2,1)}), bf16[256,16,8]{0,2,1:T(8,128)(2,1)S(1)}, u32[]{:S(2)}, u32[]{:S(2)}) async-start(bf16[256,16,8]{0,2,1:T(8,128)(2,1)} %bitcast.103), calls=%async_computation.1 | async-start | bytes 131072 | tf_op jit(solution)/shard_map/all_to_all | solution.py:42
  33.2 81.6 %all-to-all-start = ((bf16[256,16,512]{0,2,1:T(8,128)(2,1)}), bf16[256,16,512]{0,2,1:T(8,128)(2,1)}, u32[]{:S(2)}, u32[]{:S(2)}) async-start(bf16[256,16,512]{0,2,1:T(8,128)(2,1)} %bitcast.134), calls=%async_computation | async-start | bytes 8388608 | tf_op jit(solution)/shard_map/all_to_all | solution.py:40
  39.5 270.1 %all-gather.10.cloned.1.call-start = ((), (), s32[]{:S(2)}) async-start(), calls=%async_computation.6 | async-start | bytes 2228224 | tf_op jit(solution)/shard_map/all_gather | solution.py:15
  261.6 9.9 %copy-start.1 = (u32[256]{0:T(256)S(1)}, u32[256]{0:T(256)}, u32[]{:S(2)}) copy-start(u32[256]{0:T(256)} %constant.87) | copy-start | bytes 3076
  261.6 11.1 %copy-start = (f32[128]{0:T(128)S(1)}, f32[128]{0:T(128)}, u32[]{:S(2)}) copy-start(f32[128]{0:T(128)} %param.17) | copy-start | bytes 1540
Sparse Core Ops, SparseCore 0:
  9.8 115.7 all-gather.5
  128.0 71.6 all-gather.7
  271.6 37.8 all-gather.9
where the time goes:
time: 424 us; the launch traced here: 422 us
  waiting for transfers between devices  138 us (33%)
  blocking collectives  81.1 us (19%)
  matrix products  66.9 us (16%)
  local copies, waits for them, and re-layouts  60.3 us (14%)
  other arithmetic  43.7 us (10%)
  starting transfers between devices  16.6 us (4%)
  between operations  14 us (3%)
    all_to_all x1, waiting for transfers between devices, shards(): lax.all_to_all(features, 'head', split_axis=1, concat_axis=0, tiled=True)  65.2 us
    all_to_all x1, blocking collectives, shards(): lax.all_to_all(mixed_rows, 'head', split_axis=0, concat_axis=1, tiled=True)  57.4 us
    all_gather x1, waiting for transfers between devices, shards(): lax.all_gather(inject, 'head', axis=0, tiled=True)  54.1 us
    dot_general x8, matrix products, span_terms(): jnp.einsum('ghij,jghp->ighp', weights, drive_c, preferred_element_type=jn...  37.3 us
    unnamed x1, blocking collectives  23.8 us
    convert_element_type x2, local copies, waits for them, and re-layouts, shards(): regrouped.reshape(seq_rows, local_heads, HEAD_DIM).astype(jnp.float32)  17.9 us
    all_to_all x3, local copies, waits for them, and re-layouts, shards(): lax.all_to_all(mixed_rows, 'head', split_axis=0, concat_axis=1, tiled=True)  17.1 us
    dot_general x8, matrix products, span_terms(): jnp.einsum('jghp,jgn->ghpn', scaled, inject_c, preferred_element_type=jnp...  16.4 us
  transfers between devices with their start and end apart: 6, of which 5 were waited for; matrix products, arithmetic and copies ran while one was open for 12% of the time, Pallas kernels for 0%

commit v1 on v0

--- a/solution.py
+++ b/solution.py
@@ -2,11 +2,15 @@
 import jax.numpy as jnp
 from jax import lax
 from jax.sharding import PartitionSpec as P
+from jax.lax import all_to_all, axis_size
 
 HEAD_DIM = 64
 STATE = 128
 GROUPS = 8
 SPAN = 512
+mark_copies = lambda sheet: jnp.concatenate(
+    all_to_all(jnp.stack(axis_size("head") * [sheet]), "head", 0, 0), axis=0
+)
 
 
 def entering_2(x, axis, join, neutral):
@@ -47,7 +51,7 @@
         ).astype(log_decay.dtype),
     )
     inject_all, readout_all = (
-        lax.all_gather(inject, "head", axis=0, tiled=True),
+        mark_copies(inject),
         lax.all_gather(readout, "head", axis=0, tiled=True),
     )
     first_col = head_index * local_heads // group_heads * STATE

time: 424 us -> 457 us (1.078)
  blocking collectives: 81.1 us -> 170 us
  waiting for transfers between devices: 138 us -> 77.6 us
    all_to_all x0 -> x1, blocking collectives: none -> 84 us  [shards(): lax.all_to_all(features, 'head', split_axis=1, concat_axis=0, tiled=True)]
    all_gather x1 -> x0, waiting for transfers between devices: 54.1 us -> none  [shards(): lax.all_gather(inject, 'head', axis=0, tiled=True)]
    all_to_all x1, waiting for transfers between devices: 65.2 us -> 58 us  [all_to_all(jnp.stack(axis_size('head') * [sheet]), 'head', 0, 0)]
    unnamed x1, blocking collectives: 23.8 us -> 28.7 us
    unnamed x11 -> x13, local copies, waits for them, and re-layouts: 14.1 us -> 14.2 us
  transfers between devices with their start and end apart: 6 -> 5, of which waited for: 5 -> 4; matrix products, arithmetic and copies ran while one was open for 12% -> 12% of each run, Pallas kernels for 0% -> 0%
where the time goes in v1:
time: 457 us; the launch traced here: 455 us
  blocking collectives  170 us (37%)
  waiting for transfers between devices  77.6 us (17%)
  matrix products  67.2 us (15%)
  local copies, waits for them, and re-layouts  64.8 us (14%)
  other arithmetic  43.2 us (9%)
  starting transfers between devices  16.2 us (4%)
  between operations  14.3 us (3%)
    all_to_all x1, blocking collectives, shards(): lax.all_to_all(features, 'head', split_axis=1, concat_axis=0, tiled=True)  84 us
    all_to_all x1, waiting for transfers between devices, all_to_all(jnp.stack(axis_size('head') * [sheet]), 'head', 0, 0)  58 us
    all_to_all x1, blocking collectives, shards(): lax.all_to_all(mixed_rows, 'head', split_axis=0, concat_axis=1, tiled=True)  57.6 us
    dot_general x8, matrix products, span_terms(): jnp.einsum('ghij,jghp->ighp', weights, drive_c, preferred_element_type=jn...  37.4 us
    unnamed x1, blocking collectives  28.7 us
    convert_element_type x2, local copies, waits for them, and re-layouts, shards(): regrouped.reshape(seq_rows, local_heads, HEAD_DIM).astype(jnp.float32)  17.9 us
    all_to_all x3, local copies, waits for them, and re-layouts, shards(): lax.all_to_all(mixed_rows, 'head', split_axis=0, concat_axis=1, tiled=True)  17.1 us
    dot_general x8, matrix products, span_terms(): jnp.einsum('jghp,jgn->ghpn', scaled, inject_c, preferred_element_type=jnp...  16.6 us
  transfers between devices with their start and end apart: 5, of which 4 were waited for; matrix products, arithmetic and copies ran while one was open for 12% of the time, Pallas kernels for 0%

profile of v1, /device:TPU:225, one launch (start us, length us, event | category | flops | bytes accessed | tf_op | source)
XLA Modules:
  0.0 454.5 jit_solution(6791503861876137452)
XLA Ops:
  7.3 1.6 copy.82
  8.9 6.8 %all-to-all-start.2 = ((bf16[256,16,8]{0,2,1:T(8,128)(2,1)}), bf16[256,16,8]{0,2,1:T(8,128)(2,1)S(1)}, u32[]{:S(2)}, u32[]{:S(2)}) async-start(bf16[256,16,8]{0,2,1:T(8,128)(2,1)} %bitcast.103), calls=%async_computation.2 | async-start | bytes 131072 | tf_op jit(solution)/shard_map/all_to_all | solution.py:49
  15.7 1.6 copy.80
  17.3 4.9 %all-to-all-done.2 = bf16[256,16,8]{0,2,1:T(8,128)(2,1)S(1)} async-done(((bf16[256,16,8]{0,2,1:T(8,128)(2,1)}), bf16[256,16,8]{0,2,1:T(8,128)(2,1)S(1)}, u32[]{:S(2)}, u32[]{:S(2)}) %all-to-all-start.2) | async-done | bytes 65568 | tf_op jit(solution)/shard_map/all_to_all | solution.py:49
  22.2 3.5 all-to-all-start.1
  25.7 6.4 %copy.78 = bf16[256,8192]{0,1:T(8,128)(2,1)} copy(bf16[256,8192]{1,0:T(8,128)(2,1)} %param.12) | data formatting | bytes 8388608 | tf_op args[0]
  32.5 84.0 %all_to_all.63 = bf16[256,16,512]{0,2,1:T(8,128)(2,1)} all-to-all(bf16[256,16,512]{0,2,1:T(8,128)(2,1)} %bitcast.135), channel_id=1, replica_groups=mesh['seq'=16,'head'=16] {'head'}, dimensions={1} | all-to-all | bytes 8388608 | tf_op jit(solution)/shard_map/all_to_all | solution.py:44
  116.5 4.3 stack.2
  120.8 5.9 %all-to-all-start.3 = ((bf16[16,256,1024]{2,1,0:T(8,128)(2,1)}), bf16[16,256,1024]{2,1,0:T(8,128)(2,1)}, u32[]{:S(2)}, u32[]{:S(2)}) async-start(bf16[16,256,1024]{2,1,0:T(8,128)(2,1)} %stack.2), calls=%async_computation.3 | async-start | bytes 16777216 | tf_op jit(solution)/shard_map/all_to_all | solution.py:12
  126.8 9.0 %reduce-window.6 = f32[8,8,4,128]{3,1,2,0:T(8,128)S(1)} reduce-window(f32[8,8,4,128]{3,1,2,0:T(8,128)S(1)} %bitcast.140, f32[]{:T(128)} %constant.75.clone.1), window={size=1x1x1x128 pad=0_0x0_0x0_0x127_0}, to_apply=%region_0.1 | reduce-window | flops 4161536 | bytes 262148 | tf_op jit(solution)/shard_map/reduce-window
  136.7 3.1 convert_bitcast_fusion
  139.8 8.0 %copy.79 = f32[16,256,512]{1,0,2:T(8,128)} copy(f32[16,256,512]{1,2,0:T(8,128)S(1)} %convert_bitcast_fusion) | data formatting | bytes 16777216 | tf_op jit(solution)/shard_map/convert_element_type | solution.py:63
  147.9 9.8 %reshape.184 = f32[8,512,1,8,64]{1,0,4,3,2:T(8,128)} reshape(f32[16,256,512]{1,0,2:T(8,128)} %copy.79) | data formatting | bytes 16777216 | tf_op jit(solution)/shard_map/convert_element_type | solution.py:63
  157.7 4.6 %multiply_convert_fusion.7 = bf16[8,512,1,8,64]{1,0,4,3,2:T(8,128)(2,1)S(1)} fusion(f32[8,512,1,8,64]{1,0,4,3,2:T(8,128)} %reshape.184, f32[8,512,8]{1,0,2:T(8,128)S(1)} %copy.81), kind=kLoop, calls=%fused_computation.43 | loop fusion | flops 4194304 | bytes 12713984 | tf_op jit(solution)/shard_map/convert_element_type | solution.py:65
  162.3 3.5 copy.85
  165.9 58.0 %all-to-all-done.3 = bf16[16,256,1024]{2,1,0:T(8,128)(2,1)} async-done(((bf16[16,256,1024]{2,1,0:T(8,128)(2,1)}), bf16[16,256,1024]{2,1,0:T(8,128)(2,1)}, u32[]{:S(2)}, u32[]{:S(2)}) %all-to-all-start.3) | async-done | bytes 8388640 | tf_op jit(solution)/shard_map/all_to_all | solution.py:12
  223.8 1.3 constant_dynamic-slice_fusion.1
  225.2 1.3 constant_dynamic-slice_fusion.2
  226.5 1.7 broadcast.57.clone
  228.1 59.3 %while.40 = (s32[]{:T(128)}, f32[8,512,1,8,64]{1,4,3,2,0:T(8,128)}, f32[8,8,64,128]{3,2,1,0:T(8,128)}, bf16[8,512,1,8,64]{1,4,3,2,0:T(8,128)(2,1)}, f32[8,512,8]...) while((s32[]{:T(128)}, f32[8,512,1,8,64]{1,4,3,2,0:T(8,128)}, ...), condition=%wide.region_3.4_spmd.clone.clone, body=%wide.region_2.3_spmd.clone.clone.sunk | while | flops 414191616 | bytes 5492413 | solution.py:96
  228.5 4.7 %fusion.52 = f32[8,512,1,8,64]{1,4,3,2,0:T(8,128)} fusion(f32[8,512,1,8,64]{1,4,3,2,0:T(8,128)} %get-tuple-element.377, s32[]{:T(128)} %get-tuple-element.376, f32[512,512]{1,0:T(8,128)S(1)} %fusion.51, f32[8,512]{1,0:T(8,128)S(1)} %dynamic-slice_bitcast_fusion.2, pred[512,512]{1,0:T(8,128)(4,1)S(1)} %iota_compare_fusion.2, ...), kind=kOutput, calls=%fused_computation.12.clone.1 | convolution fusion | flops 278921216 | bytes 2917376 | tf_op jit(solution)/shard_map/while/body/eval_jaxpr/ghij,jghp->ighp/dot_general | solution.py:85
  233.4 2.1 fusion.54
  235.9 4.7 %fusion.52 = f32[8,512,1,8,64]{1,4,3,2,0:T(8,128)} fusion(f32[8,512,1,8,64]{1,4,3,2,0:T(8,128)} %get-tuple-element.377, s32[]{:T(128)} %get-tuple-element.376, f32[512,512]{1,0:T(8,128)S(1)} %fusion.51, f32[8,512]{1,0:T(8,128)S(1)} %dynamic-slice_bitcast_fusion.2, pred[512,512]{1,0:T(8,128)(4,1)S(1)} %iota_compare_fusion.2, ...), kind=kOutput, calls=%fused_computation.12.clone.1 | convolution fusion | flops 278921216 | bytes 2917376 | tf_op jit(solution)/shard_map/while/body/eval_jaxpr/ghij,jghp->ighp/dot_general | solution.py:85
  240.9 2.0 fusion.54
  243.3 4.7 %fusion.52 = f32[8,512,1,8,64]{1,4,3,2,0:T(8,128)} fusion(f32[8,512,1,8,64]{1,4,3,2,0:T(8,128)} %get-tuple-element.377, s32[]{:T(128)} %get-tuple-element.376, f32[512,512]{1,0:T(8,128)S(1)} %fusion.51, f32[8,512]{1,0:T(8,128)S(1)} %dynamic-slice_bitcast_fusion.2, pred[512,512]{1,0:T(8,128)(4,1)S(1)} %iota_compare_fusion.2, ...), kind=kOutput, calls=%fused_computation.12.clone.1 | convolution fusion | flops 278921216 | bytes 2917376 | tf_op jit(solution)/shard_map/while/body/eval_jaxpr/ghij,jghp->ighp/dot_general | solution.py:85
  248.3 2.1 fusion.54
  250.8 4.6 %fusion.52 = f32[8,512,1,8,64]{1,4,3,2,0:T(8,128)} fusion(f32[8,512,1,8,64]{1,4,3,2,0:T(8,128)} %get-tuple-element.377, s32[]{:T(128)} %get-tuple-element.376, f32[512,512]{1,0:T(8,128)S(1)} %fusion.51, f32[8,512]{1,0:T(8,128)S(1)} %dynamic-slice_bitcast_fusion.2, pred[512,512]{1,0:T(8,128)(4,1)S(1)} %iota_compare_fusion.2, ...), kind=kOutput, calls=%fused_computation.12.clone.1 | convolution fusion | flops 278921216 | bytes 2917376 | tf_op jit(solution)/shard_map/while/body/eval_jaxpr/ghij,jghp->ighp/dot_general | solution.py:85
  255.7 2.1 fusion.54
  258.2 4.7 %fusion.52 = f32[8,512,1,8,64]{1,4,3,2,0:T(8,128)} fusion(f32[8,512,1,8,64]{1,4,3,2,0:T(8,128)} %get-tuple-element.377, s32[]{:T(128)} %get-tuple-element.376, f32[512,512]{1,0:T(8,128)S(1)} %fusion.51, f32[8,512]{1,0:T(8,128)S(1)} %dynamic-slice_bitcast_fusion.2, pred[512,512]{1,0:T(8,128)(4,1)S(1)} %iota_compare_fusion.2, ...), kind=kOutput, calls=%fused_computation.12.clone.1 | convolution fusion | flops 278921216 | bytes 2917376 | tf_op jit(solution)/shard_map/while/body/eval_jaxpr/ghij,jghp->ighp/dot_general | solution.py:85
  263.1 2.1 fusion.54
  265.6 4.7 %fusion.52 = f32[8,512,1,8,64]{1,4,3,2,0:T(8,128)} fusion(f32[8,512,1,8,64]{1,4,3,2,0:T(8,128)} %get-tuple-element.377, s32[]{:T(128)} %get-tuple-element.376, f32[512,512]{1,0:T(8,128)S(1)} %fusion.51, f32[8,512]{1,0:T(8,128)S(1)} %dynamic-slice_bitcast_fusion.2, pred[512,512]{1,0:T(8,128)(4,1)S(1)} %iota_compare_fusion.2, ...), kind=kOutput, calls=%fused_computation.12.clone.1 | convolution fusion | flops 278921216 | bytes 2917376 | tf_op jit(solution)/shard_map/while/body/eval_jaxpr/ghij,jghp->ighp/dot_general | solution.py:85
  270.5 2.1 fusion.54
  273.0 4.7 %fusion.52 = f32[8,512,1,8,64]{1,4,3,2,0:T(8,128)} fusion(f32[8,512,1,8,64]{1,4,3,2,0:T(8,128)} %get-tuple-element.377, s32[]{:T(128)} %get-tuple-element.376, f32[512,512]{1,0:T(8,128)S(1)} %fusion.51, f32[8,512]{1,0:T(8,128)S(1)} %dynamic-slice_bitcast_fusion.2, pred[512,512]{1,0:T(8,128)(4,1)S(1)} %iota_compare_fusion.2, ...), kind=kOutput, calls=%fused_computation.12.clone.1 | convolution fusion | flops 278921216 | bytes 2917376 | tf_op jit(solution)/shard_map/while/body/eval_jaxpr/ghij,jghp->ighp/dot_general | solution.py:85
  278.0 2.1 fusion.54
  280.4 4.6 %fusion.52 = f32[8,512,1,8,64]{1,4,3,2,0:T(8,128)} fusion(f32[8,512,1,8,64]{1,4,3,2,0:T(8,128)} %get-tuple-element.377, s32[]{:T(128)} %get-tuple-element.376, f32[512,512]{1,0:T(8,128)S(1)} %fusion.51, f32[8,512]{1,0:T(8,128)S(1)} %dynamic-slice_bitcast_fusion.2, pred[512,512]{1,0:T(8,128)(4,1)S(1)} %iota_compare_fusion.2, ...), kind=kOutput, calls=%fused_computation.12.clone.1 | convolution fusion | flops 278921216 | bytes 2917376 | tf_op jit(solution)/shard_map/while/body/eval_jaxpr/ghij,jghp->ighp/dot_general | solution.py:85
  285.3 2.1 fusion.54
  287.6 8.9 %while.41 = (s32[]{:T(128)}, f32[8,64,128]{2,1,0:T(8,128)S(1)}, f32[8,8,64,128]{3,2,1,0:T(8,128)S(1)}, f32[8,8]{1,0:T(8,128)S(1)}, f32[8,8,64,128]{3,2,1,0:T(8,128)}, /*index=5*/s32[]{:T(128)}, s32[]{:T(128)}) while((s32[]{:T(128)}, f32[8,64,128]{2,1,0:T(8,128)S(1)}, f32[8,8,64,128]{3,2,1,0:T(8,128)S(1)}, f32[8,8]{1,0:T(8,128)S(1)}, ...), condition=%wide.region_5.6_spmd.clone, body=%wide.region_4.5_spmd.clone.sunk | while | flops 262147 | bytes 1310916 | solution.py:105
  287.7 1.0 bitcast_add_fusion.2
  288.8 1.0 bitcast_add_fusion.2
  289.9 1.0 bitcast_add_fusion.2
  291.1 1.0 bitcast_add_fusion.2
  292.2 1.0 bitcast_add_fusion.2
  293.3 1.0 bitcast_add_fusion.2
  294.4 1.0 bitcast_add_fusion.2
  295.5 1.0 bitcast_add_fusion.2
  299.1 28.7 %all-reduce = bf16[128]{0:T(256)(128)(2,1)S(1)} all-reduce(bf16[128]{0:T(256)(128)(2,1)S(1)} %dynamic-update-slice), channel_id=2, replica_groups=mesh['seq'=16,'head'=16] {'seq'}, use_global_device_ids=true, to_apply=%add | all-reduce | flops 128 | bytes 512
  327.9 13.5 %all-gather.7.cloned.1.call-done = bf16[128,64,128]{2,1,0:T(8,128)(2,1)} async-done(((bf16[8,64,128]{2,1,0:T(8,128)(2,1)}), bf16[128,64,128]{2,1,0:T(8,128)(2,1)}) %all-gather.7.cloned.1.call-update) | async-done | bytes 2097168 | tf_op jit(solution)/shard_map/all_gather | solution.py:19
  341.5 16.0 %while.39 = (s32[]{:T(128)}, f32[8,64,128]{2,1,0:T(8,128)S(1)}, s32[]{:T(128)}, bf16[16,8]{1,0:T(8,128)(2,1)S(1)}, bf16[16,8,64,128]{3,2,1,0:T(8,128)(2,1)}, /*index=5*/s32[]{:T(128)}, s32[]{:T(128)}, s32[]{:T(128)}) while((s32[]{:T(128)}, f32[8,64,128]{2,1,0:T(8,128)S(1)}, s32[]{:T(128)}, bf16[16,8]{1,0:T(8,128)(2,1)S(1)}, ...), condition=%wide.region_9.10_spmd, body=%wide.region_8.9_spmd.sunk | while | flops 196621 | bytes 655567 | solution.py:33
  341.5 1.0 convert_add_fusion.2
  342.6 1.0 convert_add_fusion.2
  343.7 1.0 convert_add_fusion.2
  344.7 1.0 convert_add_fusion.2
  345.8 1.0 convert_add_fusion.2
  346.9 1.0 convert_add_fusion.2
  347.9 1.0 convert_add_fusion.2
  349.0 1.0 convert_add_fusion.2
  352.2 1.0 convert_add_fusion.2
  353.3 1.0 convert_add_fusion.2
  357.5 10.9 %fusion.29 = bf16[8,512,1,8,64]{1,4,3,0,2:T(8,128)(2,1)S(1)} fusion(f32[8,512,1,8,64]{1,4,3,2,0:T(8,128)} %get-tuple-element.123, f32[8,512,1,8,64]{1,0,4,3,2:T(8,128)} %reshape.184, f32[8]{0:T(128)S(1)} %dynamic_slice.44, f32[8,512,8]{1,2,0:T(8,128)S(1)} %get-tuple-element.260, bf16[8,512,128,1]{2,1,3,0:T(8,128)(2,1)S(1)} %bitcast.138, ...), kind=kOutput, calls=%fused_computation.40 | convolution fusion | flops 548929536 | bytes 24510752 | tf_op jit(solution)/shard_map/cign,cghpn->cighp/dot_general | solution.py:120
  368.4 4.6 %copy.89 = bf16[8,512,1,8,64]{1,0,4,3,2:T(8,128)(2,1)} copy(bf16[8,512,1,8,64]{1,4,3,0,2:T(8,128)(2,1)S(1)} %fusion.29) | data formatting | bytes 8388608 | tf_op jit(solution)/shard_map/convert_element_type | solution.py:127
  373.0 7.1 %all_to_all.54 = bf16[16,256,512]{1,0,2:T(8,128)(2,1)} reshape(bf16[8,512,1,8,64]{1,0,4,3,2:T(8,128)(2,1)} %copy.89) | data formatting | bytes 8388608 | tf_op jit(solution)/shard_map/all_to_all | solution.py:128
  380.1 3.7 copy.90
  383.7 57.6 %all_to_all.64 = bf16[16,256,512]{1,2,0:T(8,128)(2,1)} all-to-all(bf16[16,256,512]{1,2,0:T(8,128)(2,1)S(1)} %copy.90), channel_id=1, replica_groups=mesh['seq'=16,'head'=16] {'head'}, dimensions={0} | all-to-all | bytes 8388608 | tf_op jit(solution)/shard_map/all_to_all | solution.py:128
  441.3 6.3 %copy.91 = bf16[256,8192]{1,0:T(8,128)(2,1)} copy(bf16[256,8192]{0,1:T(8,128)(2,1)} %bitcast.136) | data formatting | bytes 8388608 | tf_op jit(solution)/shard_map/all_to_all | solution.py:128
  (110 shorter events, 15.1 us)
Async XLA Ops:
  6.5 218.6 %all-gather.5.cloned.1.call-start = ((), (), s32[]{:S(2)}) async-start(), calls=%async_computation.5 | async-start | bytes 8912896 | tf_op jit(solution)/shard_map/all_gather | solution.py:55
  8.9 13.3 %all-to-all-start.2 = ((bf16[256,16,8]{0,2,1:T(8,128)(2,1)}), bf16[256,16,8]{0,2,1:T(8,128)(2,1)S(1)}, u32[]{:S(2)}, u32[]{:S(2)}) async-start(bf16[256,16,8]{0,2,1:T(8,128)(2,1)} %bitcast.103), calls=%async_computation.2 | async-start | bytes 131072 | tf_op jit(solution)/shard_map/all_to_all | solution.py:49
  22.2 10.3 %all-to-all-start.1 = ((bf16[256,16,8]{0,2,1:T(8,128)(2,1)}), bf16[256,16,8]{0,2,1:T(8,128)(2,1)S(1)}, u32[]{:S(2)}, u32[]{:S(2)}) async-start(bf16[256,16,8]{0,2,1:T(8,128)(2,1)} %bitcast.104), calls=%async_computation.1 | async-start | bytes 131072 | tf_op jit(solution)/shard_map/all_to_all | solution.py:46
  32.5 84.0 %copy-start = (bf16[256,1024]{1,0:T(8,128)(2,1)S(1)}, bf16[256,1024]{1,0:T(8,128)(2,1)}, u32[]{:S(2)}) copy-start(bf16[256,1024]{1,0:T(8,128)(2,1)} %param.15) | copy-start | bytes 1572868
  120.8 103.0 %all-to-all-start.3 = ((bf16[16,256,1024]{2,1,0:T(8,128)(2,1)}), bf16[16,256,1024]{2,1,0:T(8,128)(2,1)}, u32[]{:S(2)}, u32[]{:S(2)}) async-start(bf16[16,256,1024]{2,1,0:T(8,128)(2,1)} %stack.2), calls=%async_computation.3 | async-start | bytes 16777216 | tf_op jit(solution)/shard_map/all_to_all | solution.py:12
  126.7 214.8 %all-gather.7.cloned.1.call-start = ((), (), s32[]{:S(2)}) async-start(), calls=%async_computation.6 | async-start | bytes 2228224 | tf_op jit(solution)/shard_map/all_gather | solution.py:19
  287.4 9.9 %copy-start.2 = (u32[256]{0:T(256)S(1)}, u32[256]{0:T(256)}, u32[]{:S(2)}) copy-start(u32[256]{0:T(256)} %constant.87) | copy-start | bytes 3076
  287.4 11.2 %copy-start.1 = (f32[128]{0:T(128)S(1)}, f32[128]{0:T(128)}, u32[]{:S(2)}) copy-start(f32[128]{0:T(128)} %param.17) | copy-start | bytes 1540
Sparse Core Ops, SparseCore 0:
  9.8 111.3 all-gather.4
  297.4 44.0 all-gather.6
